TPU v7x, 32 devices: a whole 2x2x4 slice. The times are simulated.
32 devices in a mesh: dp: 8 (over z, x), tensor: 4 (over y, core).
Axes of the slice: x: 2, y: 2, z: 4, core: 2. Of those that a mesh axis runs over, the one named last changes fastest.
Arguments:
- layer_input: bfloat16 [8192, 512], P(('dp', 'tensor')), may hold values from -6 to 6
- segments: int32 [8, 1024], P('dp'), may hold values from 0 to 3, never falling along the last dimension, each value on 1 to 800 neighbouring positions
- norm1_gain: bfloat16 [512], replicated, may hold values from 0.5 to 1.5
- norm1_bias: bfloat16 [512], replicated, may hold values from -4 to 4
- w_query: bfloat16 [512, 512], P(None, 'tensor'), may hold values from -0.25 to 0.25
- b_query: bfloat16 [512], P('tensor'), may hold values from -6 to 6
- w_key: bfloat16 [512, 512], P(None, 'tensor'), may hold values from -0.25 to 0.25
- w_value: bfloat16 [512, 512], P(None, 'tensor'), may hold values from -0.25 to 0.25
- b_value: bfloat16 [512], P('tensor'), may hold values from -6 to 6
- w_out: bfloat16 [512, 512], P('tensor'), may hold values from -2 to 2
- b_out: bfloat16 [512], replicated, may hold values from -4 to 4
- gate1_w: bfloat16 [512, 512], P('tensor'), may hold values from -0.25 to 0.25
- gate1_b: bfloat16 [512], replicated, may hold values from -6 to 6
- norm2_gain: bfloat16 [512], replicated, may hold values from 0.5 to 1.5
- norm2_bias: bfloat16 [512], replicated, may hold values from -4 to 4
- w_in: bfloat16 [512, 2048], P(None, 'tensor'), may hold values from -0.25 to 0.25
- b_in: bfloat16 [2048], P('tensor'), may hold values from -6 to 6
- w_back: bfloat16 [2048, 512], P('tensor'), may hold values from -0.1875 to 0.1875
- b_back: bfloat16 [512], replicated, may hold values from -4 to 4
- gate2_w: bfloat16 [512, 512], P('tensor'), may hold values from -0.25 to 0.25
- gate2_b: bfloat16 [512], replicated, may hold values from -6 to 6
- cotangent: bfloat16 [8192, 512], P(('dp', 'tensor')), may hold values from -6 to 6
Outputs:
- output: bfloat16 [8192, 512], P(('dp', 'tensor'))
- input_grad: float32 [8192, 512], P(('dp', 'tensor'))
- grad_norm1_gain: float32 [512], replicated
- grad_norm1_bias: float32 [512], replicated
- grad_w_query: float32 [512, 512], P(None, 'tensor')
- grad_b_query: float32 [512], P('tensor')
- grad_w_key: float32 [512, 512], P(None, 'tensor')
- grad_w_value: float32 [512, 512], P(None, 'tensor')
- grad_b_value: float32 [512], P('tensor')
- grad_w_out: float32 [512, 512], P('tensor')
- grad_b_out: float32 [512], replicated
- grad_gate1_w: float32 [512, 512], P('tensor')
- grad_gate1_b: float32 [512], replicated
- grad_norm2_gain: float32 [512], replicated
- grad_norm2_bias: float32 [512], replicated
- grad_w_in: float32 [512, 2048], P(None, 'tensor')
- grad_b_in: float32 [2048], P('tensor')
- grad_w_back: float32 [2048, 512], P('tensor')
- grad_b_back: float32 [512], replicated
- grad_gate2_w: float32 [512, 512], P('tensor')
- grad_gate2_b: float32 [512], replicated
Inputs may be any that keep to these rules, and one draw needn't show every extreme that they name: `segments`: document numbers never fall along a sequence; every sequence holds 4 documents, none longer than 800 tokens, and one document reaches that length.
All inputs are finite; a program needn't handle non-finite values.
Results may differ from a plain program's by a relative error of at most 0.014.
Values may be sent and summed in bfloat16 or wider, within the bound.
No kernel may reach another device: no remote copies, remote signals or barrier semaphores. Data moves between devices by JAX's collectives and lax.ppermute only.
A program may use at most 64 MiB of HBM per device.

v0:
```python
import jax
import jax.numpy as jnp
from jax import lax
from jax.sharding import PartitionSpec as P

HD = 64
EPSILON = 1e-05


def matmul(left, right):
    return jnp.dot(left, right, preferred_element_type=jnp.float32)


def inner_left(left, right):
    return lax.dot_general(
        left, right, (((0,), (0,)), ((), ())), preferred_element_type=jnp.float32
    )


def outer_right(left, right):
    return lax.dot_general(
        left, right, (((1,), (1,)), ((), ())), preferred_element_type=jnp.float32
    )


def column_sum(matrix):
    return jnp.sum(matrix, axis=0, dtype=jnp.float32)


def place_columns(full, piece, start):
    current = lax.dynamic_slice_in_dim(full, start, piece.shape[1], 1)
    return lax.dynamic_update_slice_in_dim(full, current + piece, start, 1)


def smooth_unit(values):
    return jax.nn.gelu(values, approximate=True)


def norm_forward(values, gain, shift):
    centred = values - jnp.mean(values, axis=-1, keepdims=True)
    spread = jnp.mean(centred * centred, axis=-1, keepdims=True)
    inverse = lax.rsqrt(spread + EPSILON)
    unit = centred * inverse
    return (unit * gain + shift, unit, inverse)


def norm_backward(share_grad, unit, inverse, gain):
    scaled = share_grad * gain
    grad_gain = jnp.sum(share_grad * unit, axis=0)
    grad_shift = jnp.sum(share_grad, axis=0)
    average = jnp.mean(scaled, axis=-1, keepdims=True)
    project = jnp.mean(scaled * unit, axis=-1, keepdims=True)
    return (inverse * (scaled - average - unit * project), grad_gain, grad_shift)


def head_major(matrix):
    return matrix.reshape(matrix.shape[0], -1, HD).transpose(1, 0, 2)


def row_major(heads_array):
    return heads_array.transpose(1, 0, 2).reshape(heads_array.shape[1], -1)


def split_blocks(heads_array, count, block):
    return heads_array.reshape(heads_array.shape[0], count, block, HD).transpose(1, 0, 2, 3)


def join_blocks(blocks):
    count, heads, block, width = blocks.shape
    return blocks.transpose(0, 2, 1, 3).reshape(count * block, heads * width)


def build_mask(segment_row):
    places = lax.iota(jnp.int32, segment_row.shape[0])
    same_doc = segment_row[:, None] == segment_row[None, :]
    return same_doc & (places[None, :] <= places[:, None])


def attention_forward(query, keys, values, allowed):
    rows = query.shape[0]
    block = min(512, rows)
    count = rows // block
    scale_factor = HD ** (-0.5)
    heads_k = head_major(keys)
    heads_v = head_major(values)
    query_blocks = split_blocks(head_major(query), count, block)
    mask_blocks = allowed.reshape(count, block, rows)

    def one_block(pieces):
        query_block, mask_block = pieces
        scores = (
            jnp.einsum("hqd,hkd->hqk", query_block, heads_k, preferred_element_type=jnp.float32)
            * scale_factor
        )
        scores = jnp.where(mask_block[None], scores, -1e30)
        totals = jax.nn.logsumexp(scores, axis=-1, keepdims=True)
        probs = jnp.exp(scores - totals).astype(jnp.bfloat16)
        mixed = jnp.einsum("hqk,hkd->hqd", probs, heads_v, preferred_element_type=jnp.float32)
        return (mixed, totals)

    mixed, totals = lax.map(one_block, (query_blocks, mask_blocks))
    return (join_blocks(mixed).astype(jnp.bfloat16), totals)


def attention_backward(query, keys, values, allowed, totals, attended_grad):
    rows = query.shape[0]
    block = min(512, rows)
    count = rows // block
    scale_factor = HD ** (-0.5)
    heads_k = head_major(keys)
    heads_v = head_major(values)
    query_blocks = split_blocks(head_major(query), count, block)
    grad_blocks = split_blocks(head_major(attended_grad), count, block)
    mask_blocks = allowed.reshape(count, block, rows)

    def one_block(carry, pieces):
        key_acc, value_acc = carry
        query_block, grad_block, mask_block, total_block = pieces
        scores = (
            jnp.einsum("hqd,hkd->hqk", query_block, heads_k, preferred_element_type=jnp.float32)
            * scale_factor
        )
        scores = jnp.where(mask_block[None], scores, -1e30)
        probs = jnp.exp(scores - total_block)
        prob_low = probs.astype(jnp.bfloat16)
        prob_grad = jnp.einsum(
            "hqd,hkd->hqk", grad_block, heads_v, preferred_element_type=jnp.float32
        )
        weighted = jnp.sum(probs * prob_grad, axis=-1, keepdims=True)
        score_grad = (probs * (prob_grad - weighted)).astype(jnp.bfloat16)
        query_part = (
            jnp.einsum("hqk,hkd->hqd", score_grad, heads_k, preferred_element_type=jnp.float32)
            * scale_factor
        )
        key_acc = (
            key_acc
            + jnp.einsum(
                "hqk,hqd->hkd", score_grad, query_block, preferred_element_type=jnp.float32
            )
            * scale_factor
        )
        value_acc = value_acc + jnp.einsum(
            "hqk,hqd->hkd", prob_low, grad_block, preferred_element_type=jnp.float32
        )
        return ((key_acc, value_acc), query_part.astype(jnp.bfloat16))

    empty = jnp.zeros(heads_k.shape, jnp.float32)
    (key_acc, value_acc), query_parts = lax.scan(
        one_block, (empty, empty), (query_blocks, grad_blocks, mask_blocks, totals)
    )
    return (
        join_blocks(query_parts),
        row_major(key_acc).astype(jnp.bfloat16),
        row_major(value_acc).astype(jnp.bfloat16),
    )


def forward_pass(layer_input, segments, weights):
    (
        norm1_gain,
        norm1_bias,
        w_query,
        b_query,
        w_key,
        w_value,
        b_value,
        w_out,
        b_out,
        gate1_w,
        gate1_b,
        norm2_gain,
        norm2_bias,
        w_in,
        b_in,
        w_back,
        b_back,
        gate2_w,
        gate2_b,
    ) = weights
    start_col = lax.axis_index("tensor") * gate1_w.shape[0]
    inputs = layer_input.astype(jnp.float32)
    normed_part, unit_one, inverse_one = norm_forward(
        inputs, norm1_gain.astype(jnp.float32), norm1_bias.astype(jnp.float32)
    )
    normed_low = normed_part.astype(jnp.bfloat16)
    normed = lax.all_gather(normed_low, "tensor", axis=0, tiled=True)
    query = (matmul(normed, w_query) + b_query.astype(jnp.float32)).astype(jnp.bfloat16)
    keys = matmul(normed, w_key).astype(jnp.bfloat16)
    values = (matmul(normed, w_value) + b_value.astype(jnp.float32)).astype(jnp.bfloat16)
    allowed = build_mask(segments[0])
    attended, totals = attention_forward(query, keys, values, allowed)
    gate_rows = lax.dynamic_slice_in_dim(normed, start_col, gate1_w.shape[0], 1)
    branch_part, logit_one = (
        lax.psum_scatter(matmul(attended, w_out), "tensor", scatter_dimension=0, tiled=True),
        lax.psum_scatter(matmul(gate_rows, gate1_w), "tensor", scatter_dimension=0, tiled=True),
    )
    branch = branch_part + b_out.astype(jnp.float32)
    gate_one = jax.nn.sigmoid(logit_one + gate1_b.astype(jnp.float32))
    middle = inputs + gate_one * branch
    normed_two_part, unit_two, inverse_two = norm_forward(
        middle, norm2_gain.astype(jnp.float32), norm2_bias.astype(jnp.float32)
    )
    normed_two = lax.all_gather(normed_two_part.astype(jnp.bfloat16), "tensor", axis=0, tiled=True)
    hidden_input = matmul(normed_two, w_in) + b_in.astype(jnp.float32)
    hidden = smooth_unit(hidden_input).astype(jnp.bfloat16)
    gate_rows_two = lax.dynamic_slice_in_dim(normed_two, start_col, gate2_w.shape[0], 1)
    ffn_part, logit_two = (
        lax.psum_scatter(matmul(hidden, w_back), "tensor", scatter_dimension=0, tiled=True),
        lax.psum_scatter(matmul(gate_rows_two, gate2_w), "tensor", scatter_dimension=0, tiled=True),
    )
    ffn_out = ffn_part + b_back.astype(jnp.float32)
    gate_two = jax.nn.sigmoid(logit_two + gate2_b.astype(jnp.float32))
    result = middle + gate_two * ffn_out
    saved = (
        normed,
        normed_low,
        query,
        keys,
        values,
        allowed,
        attended,
        totals,
        branch,
        gate_one,
        unit_one,
        inverse_one,
        normed_two,
        hidden,
        hidden_input,
        ffn_out,
        gate_two,
        unit_two,
        inverse_two,
    )
    return (result, saved)


def body(
    layer_input,
    segments,
    norm1_gain,
    norm1_bias,
    w_query,
    b_query,
    w_key,
    w_value,
    b_value,
    w_out,
    b_out,
    gate1_w,
    gate1_b,
    norm2_gain,
    norm2_bias,
    w_in,
    b_in,
    w_back,
    b_back,
    gate2_w,
    gate2_b,
    cotangent,
):
    weights = (
        norm1_gain,
        norm1_bias,
        w_query,
        b_query,
        w_key,
        w_value,
        b_value,
        w_out,
        b_out,
        gate1_w,
        gate1_b,
        norm2_gain,
        norm2_bias,
        w_in,
        b_in,
        w_back,
        b_back,
        gate2_w,
        gate2_b,
    )
    result, saved = forward_pass(layer_input, segments, weights)
    barrier = lax.optimization_barrier((layer_input, weights))
    unused, saved = forward_pass(barrier[0], segments, barrier[1])
    (
        normed,
        normed_low,
        query,
        keys,
        values,
        allowed,
        attended,
        totals,
        branch,
        gate_one,
        unit_one,
        inverse_one,
        normed_two,
        hidden,
        hidden_input,
        ffn_out,
        gate_two,
        unit_two,
        inverse_two,
    ) = saved
    start_col = lax.axis_index("tensor") * gate1_w.shape[0]
    upstream = cotangent.astype(jnp.float32)
    ffn_grad = (gate_two * upstream).astype(jnp.bfloat16)
    logit_two_grad = (upstream * ffn_out * (gate_two * (1.0 - gate_two))).astype(jnp.bfloat16)
    ffn_grad_all, logit_two_all = (
        lax.all_gather(ffn_grad, "tensor", axis=0, tiled=True),
        lax.all_gather(logit_two_grad, "tensor", axis=0, tiled=True),
    )
    grad_b_back = column_sum(ffn_grad_all)
    grad_gate2_b = column_sum(logit_two_all)
    grad_w_back = inner_left(hidden, ffn_grad_all)
    unused_value, smooth_pull = jax.vjp(smooth_unit, hidden_input)
    hidden_grad = smooth_pull(outer_right(ffn_grad_all, w_back))[0].astype(jnp.bfloat16)
    grad_w_in = inner_left(normed_two, hidden_grad)
    grad_b_in = column_sum(hidden_grad)
    rows_two = lax.dynamic_slice_in_dim(normed_two, start_col, gate2_w.shape[0], 1)
    grad_gate2_w = inner_left(rows_two, logit_two_all)
    normed_two_grad = place_columns(
        outer_right(hidden_grad, w_in), outer_right(logit_two_all, gate2_w), start_col
    )
    normed_two_share = lax.psum_scatter(normed_two_grad, "tensor", scatter_dimension=0, tiled=True)
    middle_back, grad_norm2_gain, grad_norm2_bias = norm_backward(
        normed_two_share, unit_two, inverse_two, norm2_gain.astype(jnp.float32)
    )
    middle_grad = upstream + middle_back
    ffn_grads = (grad_w_in, grad_b_in, grad_w_back, grad_b_back, grad_gate2_w, grad_gate2_b)
    branch_grad = (gate_one * middle_grad).astype(jnp.bfloat16)
    logit_one_grad = (middle_grad * branch * (gate_one * (1.0 - gate_one))).astype(jnp.bfloat16)
    grad_b_out = column_sum(branch_grad)
    grad_gate1_b = column_sum(logit_one_grad)
    branch_all, logit_one_all = (
        lax.all_gather(branch_grad, "tensor", axis=0, tiled=True),
        lax.all_gather(logit_one_grad, "tensor", axis=0, tiled=True),
    )
    grad_w_out = inner_left(attended, branch_all)
    attended_grad = outer_right(branch_all, w_out).astype(jnp.bfloat16)
    rows_one = lax.dynamic_slice_in_dim(normed, start_col, gate1_w.shape[0], 1)
    grad_gate1_w = inner_left(rows_one, logit_one_all)
    query_grad, keys_grad, values_grad = attention_backward(
        query, keys, values, allowed, totals, attended_grad
    )
    grad_w_query = inner_left(normed, query_grad)
    grad_b_query = column_sum(query_grad)
    grad_w_key = inner_left(normed, keys_grad)
    grad_w_value = inner_left(normed, values_grad)
    grad_b_value = column_sum(values_grad)
    normed_grad = (
        outer_right(query_grad, w_query)
        + outer_right(keys_grad, w_key)
        + outer_right(values_grad, w_value)
    )
    normed_grad = place_columns(normed_grad, outer_right(logit_one_all, gate1_w), start_col)
    normed_share = lax.psum_scatter(
        normed_grad.astype(jnp.bfloat16), "tensor", scatter_dimension=0, tiled=True
    ).astype(jnp.float32)
    input_back, grad_norm1_gain, grad_norm1_bias = norm_backward(
        normed_share, unit_one, inverse_one, norm1_gain.astype(jnp.float32)
    )
    input_grad = middle_grad + input_back
    norm_sums = lax.psum(
        (
            grad_norm1_gain,
            grad_norm1_bias,
            grad_norm2_gain,
            grad_norm2_bias,
            grad_b_out,
            grad_gate1_b,
        ),
        ("dp", "tensor"),
    )
    attention_grads = (
        grad_w_query,
        grad_b_query,
        grad_w_key,
        grad_w_value,
        grad_b_value,
        grad_w_out,
        grad_gate1_w,
    )
    every_grad = lax.psum(
        (
            grad_w_query,
            grad_b_query,
            grad_w_key,
            grad_w_value,
            grad_b_value,
            grad_w_out,
            grad_gate1_w,
            grad_w_in,
            grad_b_in,
            grad_w_back,
            grad_b_back,
            grad_gate2_w,
            grad_gate2_b,
        ),
        "dp",
    )
    attention_grads = every_grad[0:7]
    ffn_grads = every_grad[7:13]
    return (
        result.astype(jnp.bfloat16),
        input_grad,
        norm_sums[0],
        norm_sums[1],
        attention_grads[0],
        attention_grads[1],
        attention_grads[2],
        attention_grads[3],
        attention_grads[4],
        attention_grads[5],
        norm_sums[4],
        attention_grads[6],
        norm_sums[5],
        norm_sums[2],
        norm_sums[3],
        ffn_grads[0],
        ffn_grads[1],
        ffn_grads[2],
        ffn_grads[3],
        ffn_grads[4],
        ffn_grads[5],
    )


def solution(mesh):
    placed = (
        P(("dp", "tensor"), None),
        P("dp", None),
        P(),
        P(),
        P(None, "tensor"),
        P("tensor"),
        P(None, "tensor"),
        P(None, "tensor"),
        P("tensor"),
        P("tensor", None),
        P(),
        P("tensor", None),
        P(),
        P(),
        P(),
        P(None, "tensor"),
        P("tensor"),
        P("tensor", None),
        P(),
        P("tensor", None),
        P(),
        P(("dp", "tensor"), None),
    )
    return jax.shard_map(
        body,
        mesh=mesh,
        in_specs=placed,
        out_specs=(
            P(("dp", "tensor"), None),
            P(("dp", "tensor"), None),
            P(),
            P(),
            P(None, "tensor"),
            P("tensor"),
            P(None, "tensor"),
            P(None, "tensor"),
            P("tensor"),
            P("tensor", None),
            P(),
            P("tensor", None),
            P(),
            P(),
            P(),
            P(None, "tensor"),
            P("tensor"),
            P("tensor", None),
            P(),
            P("tensor", None),
            P(),
        ),
        check_vma=False,
    )
```

profile of v0, /device:TPU:0, one launch (start us, length us, event | category | flops | bytes accessed | tf_op | source)
XLA Modules:
  0.0 718.7 jit_solution(1008536278620861501)
XLA Ops:
  11.0 1.9 fusion.90
  16.1 1.9 fusion.52
  18.0 14.4 %all-gather.13.cloned.1.call-done = bf16[1024,512]{1,0:T(8,128)(2,1)} async-done(((bf16[256,512]{1,0:T(8,128)(2,1)}), bf16[1024,512]{1,0:T(8,128)(2,1)}) %all-gather.13.cloned.1.call-update) | async-done | bytes 1048592 | tf_op jit(solution)/shard_map/all_gather | solution.py:186
  32.5 1.8 fusion.73
  36.2 8.7 %while.38 = (s32[]{:T(128)}, bf16[2,2,512,64]{2,3,1,0:T(8,128)(2,1)}, f32[2,2,512,1]{2,1,3,0:T(2,128)S(1)}, pred[2,512,1024]{2,1,0:T(8,128)(4,1)S(1)}, bf16[2,2,...) while((s32[]{:T(128)}, ...), condition=%wide.region_18.19_spmd, body=%wide.region_15.18_spmd.sunk | while | flops 279977984 | bytes 18268324 | solution.py:101
  46.9 1.8 fusion.133
  48.9 2.7 fusion.116
  54.8 25.5 %reduce-scatter.21.cloned.1.call-done = f32[256,512]{1,0:T(8,128)} async-done(((f32[1024,512]{1,0:T(8,128)}), f32[256,512]{1,0:T(8,128)}) %reduce-scatter.21.cloned.1.call-update) | async-done | bytes 524304 | tf_op jit(solution)/shard_map/reduce_scatter | solution.py:194
  80.3 34.1 %reduce-scatter.19.cloned.1.call-done = f32[256,512]{1,0:T(8,128)} async-done(((f32[1024,512]{1,0:T(8,128)}), f32[256,512]{1,0:T(8,128)}) %reduce-scatter.19.cloned.1.call-update) | async-done | bytes 524304 | tf_op jit(solution)/shard_map/reduce_scatter | solution.py:195
  118.3 16.8 %all-gather.15.cloned.1.call-done = bf16[1024,512]{1,0:T(8,128)(2,1)} async-done(((bf16[256,512]{1,0:T(8,128)(2,1)}), bf16[1024,512]{1,0:T(8,128)(2,1)}) %all-gather.15.cloned.1.call-update) | async-done | bytes 1048592 | tf_op jit(solution)/shard_map/all_gather | solution.py:203
  135.1 2.7 fusion.112
  138.6 30.8 %reduce-scatter.23.cloned.1.call-done = f32[256,512]{1,0:T(8,128)} async-done(((f32[1024,512]{1,0:T(8,128)}), f32[256,512]{1,0:T(8,128)}) %reduce-scatter.23.cloned.1.call-update) | async-done | bytes 524304 | tf_op jit(solution)/shard_map/reduce_scatter | solution.py:209
  169.5 2.0 fusion.100
  172.8 3.4 fusion.134
  176.2 12.2 %all-gather.17.cloned.1.call-done = bf16[1024,512]{1,0:T(8,128)(2,1)} async-done(((bf16[256,512]{1,0:T(8,128)(2,1)}), bf16[1024,512]{1,0:T(8,128)(2,1)}) %all-gather.17.cloned.1.call-update) | async-done | bytes 1048592 | tf_op jit(solution)/shard_map/all_gather | solution.py:312
  188.4 5.5 convert_reduce_fusion.2
  194.8 2.0 fusion.136
  198.2 30.3 %reduce-scatter.25.cloned.1.call-done = f32[256,512]{1,0:T(8,128)} async-done(((f32[1024,512]{1,0:T(8,128)}), f32[256,512]{1,0:T(8,128)}) %reduce-scatter.25.cloned.1.call-update) | async-done | bytes 524304 | tf_op jit(solution)/shard_map/reduce_scatter | solution.py:208
  228.5 2.2 fusion.102
  230.9 3.4 fusion.135
  234.4 13.2 %all-gather.19.cloned.1.call-done = bf16[1024,512]{1,0:T(8,128)(2,1)} async-done(((bf16[256,512]{1,0:T(8,128)(2,1)}), bf16[1024,512]{1,0:T(8,128)(2,1)}) %all-gather.19.cloned.1.call-update) | async-done | bytes 1048592 | tf_op jit(solution)/shard_map/all_gather | solution.py:313
  247.6 2.7 fusion.69
  251.1 30.8 %reduce-scatter.27.cloned.1.call-done = f32[256,512]{1,0:T(8,128)} async-done(((f32[1024,512]{1,0:T(8,128)}), f32[256,512]{1,0:T(8,128)}) %reduce-scatter.27.cloned.1.call-update) | async-done | bytes 524304 | tf_op jit(solution)/shard_map/reduce_scatter | solution.py:327
  281.9 2.1 multiply_reduce_fusion.1
  284.1 3.3 convert_reduce_fusion.6
  289.6 16.1 %all-gather.21.cloned.1.call-done = bf16[1024,512]{1,0:T(8,128)(2,1)} async-done(((bf16[256,512]{1,0:T(8,128)(2,1)}), bf16[1024,512]{1,0:T(8,128)(2,1)}) %all-gather.21.cloned.1.call-update) | async-done | bytes 1048592 | tf_op jit(solution)/shard_map/all_gather | solution.py:338
  305.7 2.4 convolution_convert_fusion
  308.1 1.9 reshape.269
  310.0 1.7 copy.48
  311.7 16.5 %while.39 = (s32[]{:T(128)}, f32[2,1024,64]{1,2,0:T(8,128)}, f32[2,1024,64]{1,2,0:T(8,128)}, bf16[2,2,512,64]{2,3,1,0:T(8,128)(2,1)}, pred[2,512,1024]{2,1,0:T(8...) while((s32[]{:T(128)}, f32[2,1024,64]{1,2,0:T(8,128)}, ...), condition=%wide.region_29.30_spmd.clone, body=%wide.region_27.29_spmd.clone.sunk | while | flops 687602688 | bytes 50229632 | solution.py:148
  314.3 1.8 multiply_reduce_fusion.7
  322.5 1.8 multiply_reduce_fusion.7
  332.4 1.8 add_add_fusion
  334.2 2.7 fusion.68
  336.9 2.7 convert_element_type.273
  343.1 21.6 %reduce-scatter.29.cloned.1.call-done = bf16[256,512]{1,0:T(8,128)(2,1)} async-done(((bf16[1024,512]{1,0:T(8,128)(2,1)}), bf16[256,512]{1,0:T(8,128)(2,1)}) %reduce-scatter.29.cloned.1.call-update) | async-done | bytes 262160 | tf_op jit(solution)/shard_map/reduce_scatter | solution.py:359
  364.7 1.9 fusion.105
  366.6 2.4 fusion.93
  370.4 15.5 %all-gather.9.cloned.1.call-done = bf16[1024,512]{1,0:T(8,128)(2,1)} async-done(((bf16[256,512]{1,0:T(8,128)(2,1)}), bf16[1024,512]{1,0:T(8,128)(2,1)}) %all-gather.9.cloned.1.call-update) | async-done | bytes 1048592 | tf_op jit(solution)/shard_map/all_gather | solution.py:186
  385.9 2.4 fusion.71
  388.3 1.9 reshape.261
  390.2 1.7 copy.43
  391.9 2.7 fusion.108
  394.9 2.4 convolution_convert_fusion.2
  397.3 2.4 fusion.72
  400.4 10.8 %while.37 = (s32[]{:T(128)}, bf16[2,2,512,64]{2,3,1,0:T(8,128)(2,1)}, pred[2,512,1024]{2,1,0:T(8,128)(4,1)S(1)}, bf16[2,2,512,64]{2,3,1,0:T(8,128)(2,1)}, bf16[2...) while((s32[]{:T(128)}, bf16[2,2,512,64]{2,3,1,0:T(8,128)(2,1)}, ...), condition=%wide.region_6.7_spmd, body=%wide.region_3.0_spmd.sunk | while | flops 279973888 | bytes 19304628 | solution.py:101
  400.5 2.1 fusion.236
  405.9 2.1 fusion.236
  412.6 1.8 fusion.132
  414.5 11.7 %reduce-scatter.11.cloned.1.call-done = f32[256,512]{1,0:T(8,128)} async-done(((f32[1024,512]{1,0:T(8,128)}), f32[256,512]{1,0:T(8,128)}) %reduce-scatter.11.cloned.1.call-update) | async-done | bytes 524304 | tf_op jit(solution)/shard_map/reduce_scatter | solution.py:195
  426.2 34.0 %reduce-scatter.13.cloned.1.call-done = f32[256,512]{1,0:T(8,128)} async-done(((f32[1024,512]{1,0:T(8,128)}), f32[256,512]{1,0:T(8,128)}) %reduce-scatter.13.cloned.1.call-update) | async-done | bytes 524304 | tf_op jit(solution)/shard_map/reduce_scatter | solution.py:194
  462.9 16.8 %all-gather.11.cloned.1.call-done = bf16[1024,512]{1,0:T(8,128)(2,1)} async-done(((bf16[256,512]{1,0:T(8,128)(2,1)}), bf16[1024,512]{1,0:T(8,128)(2,1)}) %all-gather.11.cloned.1.call-update) | async-done | bytes 1048592 | tf_op jit(solution)/shard_map/all_gather | solution.py:203
  479.7 4.1 fusion.70
  484.7 2.7 fusion.106
  487.4 3.4 fusion.144
  490.8 1.7 fusion.143
  501.2 22.1 %all-reduce.1 = (f32[128]{0:T(128)}, f32[128]{0:T(128)}, f32[512]{0:T(512)}, f32[512]{0:T(512)}, f32[512]{0:T(512)}) all-reduce(f32[128]{0:T(128)S(1)} %reduce_sum.253, f32[128]{0:T(128)S(1)} %reduce_sum.255, f32[512]{0:T(512)S(1)} %copy-done.71, f32[512]{0:T(512)S(1)} %convert_reduce_fusion.1, ...), channel_id=1, replica_groups=mesh['dp'=8,'tensor'=4] {'dp'}, use_global_device_ids=true, to_apply=%region_39.40 | all-reduce | flops 1792 | bytes 14336 | tf_op jit(solution)/shard_map/psum | solution.py:386
  523.4 37.1 %all-reduce = (f32[512]{0:T(512)}, f32[512]{0:T(512)}, f32[512]{0:T(512)}, f32[512]{0:T(512)}, f32[512]{0:T(512)}, /*index=5*/f32[512]{0:T(512)}) all-reduce(f32[512]{0:T(512)S(1)} %copy-done.62, f32[512]{0:T(512)S(1)} %copy-done.63, f32[512]{0:T(512)S(1)} %copy-done.61, ...), channel_id=1, replica_groups=mesh['dp'=8,'tensor'=4] {'dp','tensor'}, use_global_device_ids=true, to_apply=%region_34.35 | all-reduce | flops 3072 | bytes 24576 | tf_op jit(solution)/shard_map/psum | solution.py:366
  560.4 2.2 add_convert_fusion.1
  562.6 139.3 %all-reduce.5.cloned.1.call-done = (f32[512,128]{1,0:T(8,128)}, f32[512,128]{1,0:T(8,128)}, f32[512,128]{1,0:T(8,128)}, f32[128,512]{1,0:T(8,128)}, f32[128,512]...) async-done(((f32[512,128]{1,0:T(8,128)}, f32[512,128]{1,0:T(8,128)}, f32[512,128]{1,0:T(8,128)}, f32[128,512]{1,0:T(8,128)}, ...) | async-done | bytes 3670032 | tf_op jit(solution)/shard_map/psum | solution.py:386
  701.9 1.8 copy.96
  703.7 1.8 copy.97
  705.4 1.7 copy.98
  707.1 1.7 copy.99
  (334 shorter events, 80.2 us)
Async XLA Ops:
  7.2 181.2 %copy-start = (bf16[512,512]{1,0:T(8,128)(2,1)S(1)}, bf16[512,512]{1,0:T(8,128)(2,1)}, u32[]{:S(2)}) copy-start(bf16[512,512]{1,0:T(8,128)(2,1)} %param.45) | copy-start | bytes 1572868
  7.2 25.2 %copy-start.23 = (bf16[512,128]{1,0:T(8,128)(2,1)S(1)}, bf16[512,128]{1,0:T(8,128)(2,1)}, u32[]{:S(2)}) copy-start(bf16[512,128]{1,0:T(8,128)(2,1)} %param.32) | copy-start | bytes 393220
  7.2 25.2 %all-gather.13.cloned.1.call-start = ((), (), s32[]{:S(2)}) async-start(), calls=%async_computation.16 | async-start | bytes 1310720 | tf_op jit(solution)/shard_map/all_gather | solution.py:186
  8.4 25.8 %copy-start.48 = (f32[256]{0:T(256)}, f32[256]{0:T(256)S(1)}, u32[]{:S(2)}) copy-start(f32[256]{0:T(256)S(1)} %broadcast_multiply_fusion.5) | copy-start | bytes 3076
  9.6 24.7 %copy-start.52 = (f32[256]{0:T(256)}, f32[256]{0:T(256)S(1)}, u32[]{:S(2)}) copy-start(f32[256]{0:T(256)S(1)} %add_rsqrt_fusion.1) | copy-start | bytes 3076
  11.0 23.5 %copy-start.25 = (bf16[512,128]{1,0:T(8,128)(2,1)S(1)}, bf16[512,128]{1,0:T(8,128)(2,1)}, u32[]{:S(2)}) copy-start(bf16[512,128]{1,0:T(8,128)(2,1)} %param.34) | copy-start | bytes 393220
  12.9 67.5 %reduce-scatter.21.cloned.1.call-start = ((), (), s32[]{:S(2)}) async-start(), calls=%async_computation.18 | async-start | bytes 2621440 | tf_op jit(solution)/shard_map/reduce_scatter | solution.py:194
  18.0 17.0 %copy-start.27 = (bf16[512,128]{1,0:T(8,128)(2,1)S(1)}, bf16[512,128]{1,0:T(8,128)(2,1)}, u32[]{:S(2)}) copy-start(bf16[512,128]{1,0:T(8,128)(2,1)} %param.35) | copy-start | bytes 393220
  32.4 2.1 copy-start.1
  36.2 10.7 %copy-start.22 = (bf16[128,512]{1,0:T(8,128)(2,1)S(1)}, bf16[128,512]{1,0:T(8,128)(2,1)}, u32[]{:S(2)}) copy-start(bf16[128,512]{1,0:T(8,128)(2,1)} %param.37) | copy-start | bytes 393220
  44.9 3.9 copy-start.6
  48.8 65.7 %reduce-scatter.19.cloned.1.call-start = ((), (), s32[]{:S(2)}) async-start(), calls=%async_computation.17 | async-start | bytes 2621440 | tf_op jit(solution)/shard_map/reduce_scatter | solution.py:195
  48.8 2.8 copy-start.65
  48.8 65.6 %copy-start.2 = (bf16[256,512]{1,0:T(8,128)(2,1)S(1)}, bf16[256,512]{1,0:T(8,128)(2,1)}, u32[]{:S(2)}) copy-start(bf16[256,512]{1,0:T(8,128)(2,1)} %param.28) | copy-start | bytes 786436
  51.6 83.6 %all-gather.15.cloned.1.call-start = ((), (), s32[]{:S(2)}) async-start(), calls=%async_computation.19 | async-start | bytes 1310720 | tf_op jit(solution)/shard_map/all_gather | solution.py:203
  52.3 63.7 %copy-start.51 = (f32[512]{0:T(512)}, f32[512]{0:T(512)S(1)}, u32[]{:S(2)}) copy-start(f32[512]{0:T(512)S(1)} %convert_element_type.253) | copy-start | bytes 6148
  114.5 2.9 copy-start.56
  114.5 2.9 copy-start.57
  116.0 21.9 %copy-start.50 = (f32[256]{0:T(256)}, f32[256]{0:T(256)S(1)}, u32[]{:S(2)}) copy-start(f32[256]{0:T(256)S(1)} %broadcast_multiply_fusion.4) | copy-start | bytes 3076
  118.2 51.2 %reduce-scatter.23.cloned.1.call-start = ((), (), s32[]{:S(2)}) async-start(), calls=%async_computation.20 | async-start | bytes 2621440 | tf_op jit(solution)/shard_map/reduce_scatter | solution.py:209
  137.9 50.5 %all-gather.17.cloned.1.call-start = ((), (), s32[]{:S(2)}) async-start(), calls=%async_computation.21 | async-start | bytes 1310720 | tf_op jit(solution)/shard_map/all_gather | solution.py:312
  171.5 57.0 %reduce-scatter.25.cloned.1.call-start = ((), (), s32[]{:S(2)}) async-start(), calls=%async_computation.22 | async-start | bytes 2621440 | tf_op jit(solution)/shard_map/reduce_scatter | solution.py:208
  196.9 50.7 %all-gather.19.cloned.1.call-start = ((), (), s32[]{:S(2)}) async-start(), calls=%async_computation.23 | async-start | bytes 1310720 | tf_op jit(solution)/shard_map/all_gather | solution.py:313
  230.7 51.2 %reduce-scatter.27.cloned.1.call-start = ((), (), s32[]{:S(2)}) async-start(), calls=%async_computation.24 | async-start | bytes 2621440 | tf_op jit(solution)/shard_map/reduce_scatter | solution.py:327
  250.3 55.4 %all-gather.21.cloned.1.call-start = ((), (), s32[]{:S(2)}) async-start(), calls=%async_computation.25 | async-start | bytes 1310720 | tf_op jit(solution)/shard_map/all_gather | solution.py:338
  281.9 5.5 copy-start.11
  288.8 45.3 %all-gather.23.cloned.1.call-start = ((), (), s32[]{:S(2)}) async-start(), calls=%async_computation.26 | async-start | bytes 1310720 | tf_op jit(solution)/shard_map/all_gather | solution.py:339
  289.6 75.1 %reduce-scatter.29.cloned.1.call-start = ((), (), s32[]{:S(2)}) async-start(), calls=%async_computation.27 | async-start | bytes 1310720 | tf_op jit(solution)/shard_map/reduce_scatter | solution.py:359
  314.2 1.8 copy-start.43
  328.2 2.5 copy-start.44
  328.2 3.1 copy-start.24
  329.4 2.5 copy-start.26
  336.9 27.8 %copy-start.49 = (f32[256]{0:T(256)S(1)}, f32[256]{0:T(256)}, u32[]{:S(2)}) copy-start(f32[256]{0:T(256)} %copy-done.48) | copy-start | bytes 3076
  336.9 27.8 %copy-start.53 = (f32[256]{0:T(256)S(1)}, f32[256]{0:T(256)}, u32[]{:S(2)}) copy-start(f32[256]{0:T(256)} %copy-done.52) | copy-start | bytes 3076
  339.6 46.3 %all-gather.9.cloned.1.call-start = ((), (), s32[]{:S(2)}) async-start(), calls=%async_computation.10 | async-start | bytes 1310720 | tf_op jit(solution)/shard_map/all_gather | solution.py:186
  369.0 57.2 %reduce-scatter.11.cloned.1.call-start = ((), (), s32[]{:S(2)}) async-start(), calls=%async_computation.11 | async-start | bytes 2621440 | tf_op jit(solution)/shard_map/reduce_scatter | solution.py:195
  394.6 65.6 %reduce-scatter.13.cloned.1.call-start = ((), (), s32[]{:S(2)}) async-start(), calls=%async_computation.12 | async-start | bytes 2621440 | tf_op jit(solution)/shard_map/reduce_scatter | solution.py:194
  412.5 1.9 copy-start.64
  412.5 1.9 copy-start.66
  412.6 1.9 copy-start.67
  414.4 48.5 %copy-start.68 = (bf16[512]{0:T(512)(128)(2,1)S(1)}, bf16[512]{0:T(512)(128)(2,1)}, u32[]{:S(2)}) copy-start(bf16[512]{0:T(512)(128)(2,1)} %param.44) | copy-start | bytes 3076
  414.4 65.3 %copy-start.21 = (bf16[512,512]{1,0:T(8,128)(2,1)S(1)}, bf16[512,512]{1,0:T(8,128)(2,1)}, u32[]{:S(2)}) copy-start(bf16[512,512]{1,0:T(8,128)(2,1)} %param.43) | copy-start | bytes 1572868
  414.4 65.3 %all-gather.11.cloned.1.call-start = ((), (), s32[]{:S(2)}) async-start(), calls=%async_computation.13 | async-start | bytes 1310720 | tf_op jit(solution)/shard_map/all_gather | solution.py:203
  461.7 22.1 %copy-start.9 = (f32[256,512]{1,0:T(8,128)}, f32[256,512]{1,0:T(8,128)S(1)}, u32[]{:S(2)}) copy-start(f32[256,512]{1,0:T(8,128)S(1)} %get-tuple-element.332) | copy-start | bytes 1572868
  462.8 97.6 %reduce-scatter.17.cloned.1.call-start = ((), (), s32[]{:S(2)}) async-start(), calls=%async_computation.15 | async-start | bytes 2621440 | tf_op jit(solution)/shard_map/reduce_scatter | solution.py:208
  483.8 76.7 %reduce-scatter.15.cloned.1.call-start = ((), (), s32[]{:S(2)}) async-start(), calls=%async_computation.14 | async-start | bytes 2621440 | tf_op jit(solution)/shard_map/reduce_scatter | solution.py:209
  487.4 214.6 %all-reduce.5.cloned.1.call-start = ((), (), s32[]{:S(2)}) async-start(), calls=%async_computation.28 | async-start | bytes 7340032 | tf_op jit(solution)/shard_map/psum | solution.py:386
  487.4 3.4 copy-start.16
  487.4 3.4 copy-start.30
  490.8 2.8 copy-start.13
  492.5 2.1 copy-start.14
  492.5 2.1 copy-start.18
  494.6 3.4 copy-start.20
  499.9 23.4 %copy-start.58 = (f32[512]{0:T(512)S(1)}, f32[512]{0:T(512)}, u32[]{:S(2)}) copy-start(f32[512]{0:T(512)} %get-tuple-element.247) | copy-start | bytes 6148
  499.9 23.4 %copy-start.59 = (f32[512]{0:T(512)S(1)}, f32[512]{0:T(512)}, u32[]{:S(2)}) copy-start(f32[512]{0:T(512)} %get-tuple-element.252) | copy-start | bytes 6148
  499.9 23.4 %copy-start.60 = (f32[512]{0:T(512)S(1)}, f32[512]{0:T(512)}, u32[]{:S(2)}) copy-start(f32[512]{0:T(512)} %get-tuple-element.324) | copy-start | bytes 6148
  499.9 23.4 %copy-start.61 = (f32[512]{0:T(512)S(1)}, f32[512]{0:T(512)}, u32[]{:S(2)}) copy-start(f32[512]{0:T(512)} %get-tuple-element.327) | copy-start | bytes 6148
  499.9 23.4 %copy-start.62 = (f32[512]{0:T(512)S(1)}, f32[512]{0:T(512)}, u32[]{:S(2)}) copy-start(f32[512]{0:T(512)} %get-tuple-element.250) | copy-start | bytes 6148
  499.9 23.4 %copy-start.63 = (f32[512]{0:T(512)S(1)}, f32[512]{0:T(512)}, u32[]{:S(2)}) copy-start(f32[512]{0:T(512)} %get-tuple-element.254) | copy-start | bytes 6148
  499.9 60.5 %copy-start.10 = (f32[256,512]{1,0:T(8,128)S(1)}, f32[256,512]{1,0:T(8,128)}, u32[]{:S(2)}) copy-start(f32[256,512]{1,0:T(8,128)} %copy-done.9) | copy-start | bytes 1572868
  701.9 6.9 copy-start.46
  701.9 7.6 %copy-start.34 = (f32[512,512]{1,0:T(8,128)S(1)}, f32[512,512]{1,0:T(8,128)}, u32[]{:S(2)}) copy-start(f32[512,512]{1,0:T(8,128)} %get-tuple-element.593) | copy-start | bytes 3145732
  703.7 6.8 copy-start.33
  709.5 1.9 copy-start.45
  (41 other events, 43.0 us)
Sparse Core Ops, SparseCore 0:
  13.0 19.4 all-gather.12
  48.9 31.4 reduce-scatter.20
  83.0 31.3 reduce-scatter.18
  118.4 16.7 all-gather.14
  138.0 31.4 reduce-scatter.22
  171.6 16.7 all-gather.16
  197.0 31.4 reduce-scatter.24
  230.8 16.7 all-gather.18
  250.5 31.4 reduce-scatter.26
  289.0 16.7 all-gather.20
  307.9 16.7 all-gather.22
  339.7 24.8 reduce-scatter.28
  369.1 16.7 all-gather.8
  394.7 31.4 reduce-scatter.10
  428.7 31.4 reduce-scatter.12
  462.9 16.7 all-gather.10
  483.9 31.4 reduce-scatter.16
  517.9 31.5 reduce-scatter.14
  555.9 145.9 all-reduce.4
where the time goes:
time: 720 us; the launch traced here: 719 us
  waiting for transfers between devices  464 us (64%)
  matrix products  87.1 us (12%)
  blocking collectives  59.2 us (8%)
  other arithmetic  56.5 us (8%)
  local copies, waits for them, and re-layouts  35.3 us (5%)
  between operations  14.7 us (2%)
    psum x1, waiting for transfers between devices, body(): lax.psum((grad_w_query, grad_b_query, grad_w_key, grad_w_value, grad_b_va...  139 us
    reduce_scatter x2, waiting for transfers between devices, forward_pass(): lax.psum_scatter(matmul(attended, w_out), 'tensor', scatter_dimension=0,...  59.5 us
    reduce_scatter x2, waiting for transfers between devices, forward_pass(): lax.psum_scatter(matmul(gate_rows, gate1_w), 'tensor', scatter_dimension=...  45.8 us
    psum x1, blocking collectives, body(): lax.psum((grad_norm1_gain, grad_norm1_bias, grad_norm2_gain, grad_norm2_b...  37.1 us
    dot_general x15, matrix products, matmul(): return jnp.dot(left, right, preferred_element_type=jnp.float32)  33.9 us
    all_gather x2, waiting for transfers between devices, forward_pass(): lax.all_gather(normed_two_part.astype(jnp.bfloat16), 'tensor', axis=0, ti...  33.6 us
    reduce_scatter x1, waiting for transfers between devices, body(): lax.psum_scatter(normed_two_grad, 'tensor', scatter_dimension=0, tiled=True)  30.8 us
    reduce_scatter x2, waiting for transfers between devices, forward_pass(): lax.psum_scatter(matmul(gate_rows_two, gate2_w), 'tensor', scatter_dimens...  30.8 us
  transfers between devices with their start and end apart: 19, of which 16 were waited for; matrix products, arithmetic and copies ran while one was open for 12% of the time, Pallas kernels for 0%

commit v1 on v0

--- a/solution.py
+++ b/solution.py
@@ -183,7 +183,14 @@
         inputs, norm1_gain.astype(jnp.float32), norm1_bias.astype(jnp.float32)
     )
     normed_low = normed_part.astype(jnp.bfloat16)
-    normed = lax.all_gather(normed_low, "tensor", axis=0, tiled=True)
+    ring = [normed_low]
+    for hop in range(3):
+        ring.append(lax.ppermute(ring[-1], "tensor", [(dev, (dev + 1) % 4) for dev in range(4)]))
+    normed = jnp.roll(
+        jnp.concatenate(ring[::-1], axis=0),
+        (lax.axis_index("tensor") + 1) * ring[0].shape[0],
+        axis=0,
+    )
     query = (matmul(normed, w_query) + b_query.astype(jnp.float32)).astype(jnp.bfloat16)
     keys = matmul(normed, w_key).astype(jnp.bfloat16)
     values = (matmul(normed, w_value) + b_value.astype(jnp.float32)).astype(jnp.bfloat16)

time: 720 us -> 710 us (0.986)
  local copies, waits for them, and re-layouts: 35.3 us -> 25.2 us
    all_gather x2 -> x0, waiting for transfers between devices: 29.9 us -> none  [forward_pass(): normed = lax.all_gather(normed_low, 'tensor', axis=0, tiled=True)]
    ppermute x0 -> x6, waiting for transfers between devices: none -> 28.5 us  [forward_pass(): lax.ppermute(ring[-1], 'tensor', [(dev, (dev + 1) % 4) for dev in range(4)])]
    unnamed x133 -> x139, local copies, waits for them, and re-layouts: 18.1 us -> 18.3 us
  transfers between devices with their start and end apart: 19 -> 23, of which waited for: 16 -> 20; matrix products, arithmetic and copies ran while one was open for 12% -> 11% of each run, Pallas kernels for 0% -> 0%
where the time goes in v1:
time: 710 us; the launch traced here: 709 us
  waiting for transfers between devices  470 us (66%)
  matrix products  85.9 us (12%)
  blocking collectives  59.3 us (8%)
  other arithmetic  51.1 us (7%)
  local copies, waits for them, and re-layouts  25.2 us (4%)
  between operations  14.9 us (2%)
    psum x1, waiting for transfers between devices, body(): lax.psum((grad_w_query, grad_b_query, grad_w_key, grad_w_value, grad_b_va...  139 us
    reduce_scatter x2, waiting for transfers between devices, forward_pass(): lax.psum_scatter(matmul(attended, w_out), 'tensor', scatter_dimension=0,...  64.4 us
    reduce_scatter x2, waiting for transfers between devices, forward_pass(): lax.psum_scatter(matmul(gate_rows, gate1_w), 'tensor', scatter_dimension=...  48.9 us
    psum x1, blocking collectives, body(): lax.psum((grad_norm1_gain, grad_norm1_bias, grad_norm2_gain, grad_norm2_b...  37.1 us
    dot_general x15, matrix products, matmul(): return jnp.dot(left, right, preferred_element_type=jnp.float32)  33.7 us
    all_gather x2, waiting for transfers between devices, forward_pass(): lax.all_gather(normed_two_part.astype(jnp.bfloat16), 'tensor', axis=0, ti...  33.6 us
    reduce_scatter x1, waiting for transfers between devices, body(): lax.psum_scatter(normed_two_grad, 'tensor', scatter_dimension=0, tiled=True)  30.8 us
    reduce_scatter x2, waiting for transfers between devices, forward_pass(): lax.psum_scatter(matmul(gate_rows_two, gate2_w), 'tensor', scatter_dimens...  30.8 us
  transfers between devices with their start and end apart: 23, of which 20 were waited for; matrix products, arithmetic and copies ran while one was open for 11% of the time, Pallas kernels for 0%

profile of v1, /device:TPU:0, one launch (start us, length us, event | category | flops | bytes accessed | tf_op | source)
XLA Modules:
  0.0 708.8 jit_solution(18176467662834618916)
XLA Ops:
  12.6 6.0 collective-permute-done.3
  21.9 2.5 collective-permute-done.4
  24.4 1.9 fusion.52
  26.3 3.9 collective-permute-done.5
  32.4 1.7 convolution_convert_fusion.1
  34.2 1.7 fusion.74
  35.9 7.3 %while.38 = (s32[]{:T(128)}, bf16[2,2,512,64]{2,3,1,0:T(8,128)(2,1)S(1)}, f32[2,2,512,1]{2,1,3,0:T(2,128)S(1)}, pred[2,512,1024]{2,1,0:T(8,128)(4,1)S(1)}, bf16[...) while((s32[]{:T(128)}, ...), condition=%wide.region_18.20_spmd, body=%wide.region_15.19_spmd.sunk | while | flops 279977984 | bytes 16171117 | solution.py:101
  43.6 1.8 fusion.151
  45.5 3.0 fusion.128
  48.7 30.3 %reduce-scatter.21.cloned.1.call-done = f32[256,512]{1,0:T(8,128)} async-done(((f32[1024,512]{1,0:T(8,128)}), f32[256,512]{1,0:T(8,128)}) %reduce-scatter.21.cloned.1.call-update) | async-done | bytes 524304 | tf_op jit(solution)/shard_map/reduce_scatter | solution.py:201
  79.0 34.2 %reduce-scatter.19.cloned.1.call-done = f32[256,512]{1,0:T(8,128)} async-done(((f32[1024,512]{1,0:T(8,128)}), f32[256,512]{1,0:T(8,128)}) %reduce-scatter.19.cloned.1.call-update) | async-done | bytes 524304 | tf_op jit(solution)/shard_map/reduce_scatter | solution.py:202
  115.8 16.8 %all-gather.9.cloned.1.call-done = bf16[1024,512]{1,0:T(8,128)(2,1)} async-done(((bf16[256,512]{1,0:T(8,128)(2,1)}), bf16[1024,512]{1,0:T(8,128)(2,1)}) %all-gather.9.cloned.1.call-update) | async-done | bytes 1048592 | tf_op jit(solution)/shard_map/all_gather | solution.py:210
  132.6 2.7 fusion.124
  136.1 30.8 %reduce-scatter.23.cloned.1.call-done = f32[256,512]{1,0:T(8,128)} async-done(((f32[1024,512]{1,0:T(8,128)}), f32[256,512]{1,0:T(8,128)}) %reduce-scatter.23.cloned.1.call-update) | async-done | bytes 524304 | tf_op jit(solution)/shard_map/reduce_scatter | solution.py:216
  166.9 1.9 fusion.103
  170.2 3.4 fusion.152
  173.5 12.2 %all-gather.11.cloned.1.call-done = bf16[1024,512]{1,0:T(8,128)(2,1)} async-done(((bf16[256,512]{1,0:T(8,128)(2,1)}), bf16[1024,512]{1,0:T(8,128)(2,1)}) %all-gather.11.cloned.1.call-update) | async-done | bytes 1048592 | tf_op jit(solution)/shard_map/all_gather | solution.py:319
  185.8 5.5 convert_reduce_fusion.2
  192.3 2.0 fusion.154
  195.7 30.3 %reduce-scatter.25.cloned.1.call-done = f32[256,512]{1,0:T(8,128)} async-done(((f32[1024,512]{1,0:T(8,128)}), f32[256,512]{1,0:T(8,128)}) %reduce-scatter.25.cloned.1.call-update) | async-done | bytes 524304 | tf_op jit(solution)/shard_map/reduce_scatter | solution.py:215
  225.9 2.1 fusion.105
  228.3 3.4 fusion.153
  231.7 13.2 %all-gather.13.cloned.1.call-done = bf16[1024,512]{1,0:T(8,128)(2,1)} async-done(((bf16[256,512]{1,0:T(8,128)(2,1)}), bf16[1024,512]{1,0:T(8,128)(2,1)}) %all-gather.13.cloned.1.call-update) | async-done | bytes 1048592 | tf_op jit(solution)/shard_map/all_gather | solution.py:320
  245.0 2.7 fusion.69
  248.4 30.8 %reduce-scatter.27.cloned.1.call-done = f32[256,512]{1,0:T(8,128)} async-done(((f32[1024,512]{1,0:T(8,128)}), f32[256,512]{1,0:T(8,128)}) %reduce-scatter.27.cloned.1.call-update) | async-done | bytes 524304 | tf_op jit(solution)/shard_map/reduce_scatter | solution.py:334
  279.3 2.0 multiply_reduce_fusion.1
  281.3 3.1 convert_reduce_fusion.6
  286.4 16.2 %all-gather.15.cloned.1.call-done = bf16[1024,512]{1,0:T(8,128)(2,1)} async-done(((bf16[256,512]{1,0:T(8,128)(2,1)}), bf16[1024,512]{1,0:T(8,128)(2,1)}) %all-gather.15.cloned.1.call-update) | async-done | bytes 1048592 | tf_op jit(solution)/shard_map/all_gather | solution.py:345
  302.7 1.7 convolution_convert_fusion
  306.2 14.3 %while.39 = (s32[]{:T(128)}, f32[2,1024,64]{1,2,0:T(8,128)S(1)}, f32[2,1024,64]{1,2,0:T(8,128)}, bf16[2,2,512,64]{2,3,1,0:T(8,128)(2,1)}, pred[2,512,1024]{2,1,0...) while((s32[]{:T(128)}, f32[2,1024,64]{1,2,0:T(8,128)S(1)}, ...), condition=%wide.region_29.31_spmd.clone, body=%wide.region_27.30_spmd.clone.sunk | while | flops 687602688 | bytes 43938064 | solution.py:148
  308.8 1.8 multiply_reduce_fusion.7
  315.9 1.8 multiply_reduce_fusion.7
  323.5 1.8 add_add_fusion
  325.3 2.6 fusion.68
  327.9 2.8 convert_element_type.273
  334.2 21.6 %reduce-scatter.29.cloned.1.call-done = bf16[256,512]{1,0:T(8,128)(2,1)} async-done(((bf16[1024,512]{1,0:T(8,128)(2,1)}), bf16[256,512]{1,0:T(8,128)(2,1)}) %reduce-scatter.29.cloned.1.call-update) | async-done | bytes 262160 | tf_op jit(solution)/shard_map/reduce_scatter | solution.py:366
  355.8 1.9 fusion.108
  357.6 2.2 fusion.96
  359.8 5.8 collective-permute-done
  365.6 5.8 collective-permute-done.1
  372.7 4.5 collective-permute-done.2
  378.7 1.8 fusion.120
  380.5 1.7 fusion.71
  383.2 1.7 copy.43
  385.2 2.4 convolution_convert_fusion.2
  387.6 2.4 fusion.72
  390.0 9.4 %while.37 = (s32[]{:T(128)}, bf16[2,2,512,64]{2,3,1,0:T(8,128)(2,1)S(1)}, pred[2,512,1024]{2,1,0:T(8,128)(4,1)S(1)}, bf16[2,2,512,64]{2,3,1,0:T(8,128)(2,1)}, bf...) while((s32[]{:T(128)}, bf16[2,2,512,64]{2,3,1,0:T(8,128)(2,1)S(1)}, ...), condition=%wide.region_6.8_spmd, body=%wide.region_3.7_spmd.sunk | while | flops 279973888 | bytes 17207420 | solution.py:101
  390.1 2.1 fusion.242
  394.8 2.1 fusion.242
  399.8 1.8 fusion.150
  401.7 14.7 %reduce-scatter.11.cloned.1.call-done = f32[256,512]{1,0:T(8,128)} async-done(((f32[1024,512]{1,0:T(8,128)}), f32[256,512]{1,0:T(8,128)}) %reduce-scatter.11.cloned.1.call-update) | async-done | bytes 524304 | tf_op jit(solution)/shard_map/reduce_scatter | solution.py:202
  416.5 34.1 %reduce-scatter.13.cloned.1.call-done = f32[256,512]{1,0:T(8,128)} async-done(((f32[1024,512]{1,0:T(8,128)}), f32[256,512]{1,0:T(8,128)}) %reduce-scatter.13.cloned.1.call-update) | async-done | bytes 524304 | tf_op jit(solution)/shard_map/reduce_scatter | solution.py:201
  453.2 16.8 %all-gather.7.cloned.1.call-done = bf16[1024,512]{1,0:T(8,128)(2,1)} async-done(((bf16[256,512]{1,0:T(8,128)(2,1)}), bf16[1024,512]{1,0:T(8,128)(2,1)}) %all-gather.7.cloned.1.call-update) | async-done | bytes 1048592 | tf_op jit(solution)/shard_map/all_gather | solution.py:210
  470.0 4.1 fusion.70
  475.0 2.7 fusion.118
  477.8 3.1 fusion.159
  480.9 1.7 fusion.158
  491.4 22.2 %all-reduce.1 = (f32[128]{0:T(128)}, f32[128]{0:T(128)}, f32[512]{0:T(512)}, f32[512]{0:T(512)}, f32[512]{0:T(512)}) all-reduce(f32[128]{0:T(128)S(1)} %reduce_sum.253, f32[128]{0:T(128)S(1)} %reduce_sum.255, f32[512]{0:T(512)S(1)} %copy-done.66, f32[512]{0:T(512)S(1)} %convert_reduce_fusion.1, ...), channel_id=1, replica_groups=mesh['dp'=8,'tensor'=4] {'dp'}, use_global_device_ids=true, to_apply=%region_39.41 | all-reduce | flops 1792 | bytes 14336 | tf_op jit(solution)/shard_map/psum | solution.py:393
  513.6 37.1 %all-reduce = (f32[512]{0:T(512)}, f32[512]{0:T(512)}, f32[512]{0:T(512)}, f32[512]{0:T(512)}, f32[512]{0:T(512)}, /*index=5*/f32[512]{0:T(512)}) all-reduce(f32[512]{0:T(512)S(1)} %copy-done.54, f32[512]{0:T(512)S(1)} %copy-done.55, f32[512]{0:T(512)S(1)} %copy-done.53, ...), channel_id=1, replica_groups=mesh['dp'=8,'tensor'=4] {'dp','tensor'}, use_global_device_ids=true, to_apply=%region_34.36 | all-reduce | flops 3072 | bytes 24576 | tf_op jit(solution)/shard_map/psum | solution.py:373
  550.7 2.3 add_convert_fusion.1
  553.0 139.0 %all-reduce.5.cloned.1.call-done = (f32[512,128]{1,0:T(8,128)}, f32[512,128]{1,0:T(8,128)}, f32[512,128]{1,0:T(8,128)}, f32[128,512]{1,0:T(8,128)}, f32[128,512]...) async-done(((f32[512,128]{1,0:T(8,128)}, f32[512,128]{1,0:T(8,128)}, f32[512,128]{1,0:T(8,128)}, f32[128,512]{1,0:T(8,128)}, ...) | async-done | bytes 3670032 | tf_op jit(solution)/shard_map/psum | solution.py:393
  692.0 1.8 copy.96
  693.8 1.8 copy.97
  697.2 1.7 copy.99
  (316 shorter events, 74.1 us)
Async XLA Ops:
  7.2 178.6 %copy-start = (bf16[512,512]{1,0:T(8,128)(2,1)S(1)}, bf16[512,512]{1,0:T(8,128)(2,1)}, u32[]{:S(2)}) copy-start(bf16[512,512]{1,0:T(8,128)(2,1)} %param.47) | copy-start | bytes 1572868
  7.2 71.8 %reduce-scatter.21.cloned.1.call-start = ((), (), s32[]{:S(2)}) async-start(), calls=%async_computation.16 | async-start | bytes 2621440 | tf_op jit(solution)/shard_map/reduce_scatter | solution.py:201
  8.4 10.2 %copy-start.42 = (f32[256]{0:T(256)}, f32[256]{0:T(256)S(1)}, u32[]{:S(2)}) copy-start(f32[256]{0:T(256)S(1)} %broadcast_multiply_fusion.5) | copy-start | bytes 3076
  9.6 9.0 %copy-start.46 = (f32[256]{0:T(256)}, f32[256]{0:T(256)S(1)}, u32[]{:S(2)}) copy-start(f32[256]{0:T(256)S(1)} %add_rsqrt_fusion.1) | copy-start | bytes 3076
  12.1 6.5 collective-permute-start.3
  18.6 5.8 collective-permute-start.4
  24.4 5.8 collective-permute-start.5
  24.4 7.3 %copy-start.17 = (bf16[512,128]{1,0:T(8,128)(2,1)S(1)}, bf16[512,128]{1,0:T(8,128)(2,1)}, u32[]{:S(2)}) copy-start(bf16[512,128]{1,0:T(8,128)(2,1)} %param.34) | copy-start | bytes 393220
  26.3 6.1 copy-start.23
  31.7 2.4 copy-start.19
  35.9 7.7 %copy-start.21 = (bf16[128,512]{1,0:T(8,128)(2,1)S(1)}, bf16[128,512]{1,0:T(8,128)(2,1)}, u32[]{:S(2)}) copy-start(bf16[128,512]{1,0:T(8,128)(2,1)} %param.39) | copy-start | bytes 393220
  45.4 67.7 %reduce-scatter.19.cloned.1.call-start = ((), (), s32[]{:S(2)}) async-start(), calls=%async_computation.15 | async-start | bytes 2621440 | tf_op jit(solution)/shard_map/reduce_scatter | solution.py:202
  45.5 3.1 copy-start.59
  45.5 3.1 copy-start.57
  45.5 3.1 copy-start.56
  45.5 3.1 copy-start.61
  45.5 67.6 %copy-start.3 = (bf16[256,512]{1,0:T(8,128)(2,1)S(1)}, bf16[256,512]{1,0:T(8,128)(2,1)}, u32[]{:S(2)}) copy-start(bf16[256,512]{1,0:T(8,128)(2,1)} %param.30) | copy-start | bytes 786436
  48.5 84.1 %all-gather.9.cloned.1.call-start = ((), (), s32[]{:S(2)}) async-start(), calls=%async_computation.17 | async-start | bytes 1310720 | tf_op jit(solution)/shard_map/all_gather | solution.py:210
  48.6 66.0 %copy-start.45 = (f32[512]{0:T(512)}, f32[512]{0:T(512)S(1)}, u32[]{:S(2)}) copy-start(f32[512]{0:T(512)S(1)} %convert_element_type.253) | copy-start | bytes 6148
  114.6 20.7 %copy-start.44 = (f32[256]{0:T(256)}, f32[256]{0:T(256)S(1)}, u32[]{:S(2)}) copy-start(f32[256]{0:T(256)S(1)} %broadcast_multiply_fusion.4) | copy-start | bytes 3076
  115.7 51.2 %copy-start.14 = (bf16[256,512]{1,0:T(8,128)(2,1)S(1)}, bf16[256,512]{1,0:T(8,128)(2,1)}, u32[]{:S(2)}) copy-start(bf16[256,512]{1,0:T(8,128)(2,1)} %param.51) | copy-start | bytes 786436
  115.8 51.2 %reduce-scatter.23.cloned.1.call-start = ((), (), s32[]{:S(2)}) async-start(), calls=%async_computation.18 | async-start | bytes 2621440 | tf_op jit(solution)/shard_map/reduce_scatter | solution.py:216
  135.4 50.4 %all-gather.11.cloned.1.call-start = ((), (), s32[]{:S(2)}) async-start(), calls=%async_computation.19 | async-start | bytes 1310720 | tf_op jit(solution)/shard_map/all_gather | solution.py:319
  168.9 57.1 %reduce-scatter.25.cloned.1.call-start = ((), (), s32[]{:S(2)}) async-start(), calls=%async_computation.20 | async-start | bytes 2621440 | tf_op jit(solution)/shard_map/reduce_scatter | solution.py:215
  194.3 50.6 %all-gather.13.cloned.1.call-start = ((), (), s32[]{:S(2)}) async-start(), calls=%async_computation.21 | async-start | bytes 1310720 | tf_op jit(solution)/shard_map/all_gather | solution.py:320
  228.1 51.2 %reduce-scatter.27.cloned.1.call-start = ((), (), s32[]{:S(2)}) async-start(), calls=%async_computation.22 | async-start | bytes 2621440 | tf_op jit(solution)/shard_map/reduce_scatter | solution.py:334
  247.7 55.0 %all-gather.15.cloned.1.call-start = ((), (), s32[]{:S(2)}) async-start(), calls=%async_computation.23 | async-start | bytes 1310720 | tf_op jit(solution)/shard_map/all_gather | solution.py:345
  279.2 5.1 copy-start.6
  285.8 39.5 %all-gather.17.cloned.1.call-start = ((), (), s32[]{:S(2)}) async-start(), calls=%async_computation.24 | async-start | bytes 1310720 | tf_op jit(solution)/shard_map/all_gather | solution.py:346
  286.4 69.4 %reduce-scatter.29.cloned.1.call-start = ((), (), s32[]{:S(2)}) async-start(), calls=%async_computation.25 | async-start | bytes 1310720 | tf_op jit(solution)/shard_map/reduce_scatter | solution.py:366
  320.5 2.1 copy-start.18
  320.6 2.5 copy-start.24
  327.9 27.8 %copy-start.43 = (f32[256]{0:T(256)S(1)}, f32[256]{0:T(256)}, u32[]{:S(2)}) copy-start(f32[256]{0:T(256)} %copy-done.42) | copy-start | bytes 3076
  327.9 27.8 %copy-start.47 = (f32[256]{0:T(256)S(1)}, f32[256]{0:T(256)}, u32[]{:S(2)}) copy-start(f32[256]{0:T(256)} %copy-done.46) | copy-start | bytes 3076
  327.9 29.7 %copy-start.8 = (f32[256,512]{1,0:T(8,128)S(1)}, f32[256,512]{1,0:T(8,128)}, u32[]{:S(2)}) copy-start(f32[256,512]{1,0:T(8,128)} %copy-done.7) | copy-start | bytes 1572868
  330.7 85.7 %reduce-scatter.11.cloned.1.call-start = ((), (), s32[]{:S(2)}) async-start(), calls=%async_computation.10 | async-start | bytes 2621440 | tf_op jit(solution)/shard_map/reduce_scatter | solution.py:202
  359.8 5.8 collective-permute-start
  365.6 5.8 collective-permute-start.1
  371.4 5.8 collective-permute-start.2
  380.5 4.6 copy-start.25
  384.9 65.7 %reduce-scatter.13.cloned.1.call-start = ((), (), s32[]{:S(2)}) async-start(), calls=%async_computation.11 | async-start | bytes 2621440 | tf_op jit(solution)/shard_map/reduce_scatter | solution.py:201
  390.0 9.7 %copy-start.22 = (bf16[128,512]{1,0:T(8,128)(2,1)S(1)}, bf16[128,512]{1,0:T(8,128)(2,1)}, u32[]{:S(2)}) copy-start(bf16[128,512]{1,0:T(8,128)(2,1)} %param.39) | copy-start | bytes 393220
  401.6 51.6 %copy-start.63 = (bf16[512]{0:T(512)(128)(2,1)S(1)}, bf16[512]{0:T(512)(128)(2,1)}, u32[]{:S(2)}) copy-start(bf16[512]{0:T(512)(128)(2,1)} %param.46) | copy-start | bytes 3076
  401.6 68.4 %copy-start.15 = (bf16[512,512]{1,0:T(8,128)(2,1)S(1)}, bf16[512,512]{1,0:T(8,128)(2,1)}, u32[]{:S(2)}) copy-start(bf16[512,512]{1,0:T(8,128)(2,1)} %param.45) | copy-start | bytes 1572868
  401.6 68.4 %all-gather.7.cloned.1.call-start = ((), (), s32[]{:S(2)}) async-start(), calls=%async_computation.12 | async-start | bytes 1310720 | tf_op jit(solution)/shard_map/all_gather | solution.py:210
  453.2 97.6 %reduce-scatter.17.cloned.1.call-start = ((), (), s32[]{:S(2)}) async-start(), calls=%async_computation.14 | async-start | bytes 2621440 | tf_op jit(solution)/shard_map/reduce_scatter | solution.py:215
  474.1 3.7 copy-start.29
  474.1 76.6 %reduce-scatter.15.cloned.1.call-start = ((), (), s32[]{:S(2)}) async-start(), calls=%async_computation.13 | async-start | bytes 2621440 | tf_op jit(solution)/shard_map/reduce_scatter | solution.py:216
  477.8 214.2 %all-reduce.5.cloned.1.call-start = ((), (), s32[]{:S(2)}) async-start(), calls=%async_computation.26 | async-start | bytes 7340032 | tf_op jit(solution)/shard_map/psum | solution.py:393
  477.8 3.1 copy-start.11
  477.8 3.1 copy-start.27
  480.9 2.8 copy-start.2
  483.7 3.5 copy-start.9
  484.9 3.6 copy-start.10
  484.9 3.6 copy-start.13
  490.1 23.4 %copy-start.50 = (f32[512]{0:T(512)S(1)}, f32[512]{0:T(512)}, u32[]{:S(2)}) copy-start(f32[512]{0:T(512)} %get-tuple-element.248) | copy-start | bytes 6148
  490.1 23.4 %copy-start.51 = (f32[512]{0:T(512)S(1)}, f32[512]{0:T(512)}, u32[]{:S(2)}) copy-start(f32[512]{0:T(512)} %get-tuple-element.253) | copy-start | bytes 6148
  490.1 23.4 %copy-start.52 = (f32[512]{0:T(512)S(1)}, f32[512]{0:T(512)}, u32[]{:S(2)}) copy-start(f32[512]{0:T(512)} %get-tuple-element.325) | copy-start | bytes 6148
  490.2 23.4 %copy-start.53 = (f32[512]{0:T(512)S(1)}, f32[512]{0:T(512)}, u32[]{:S(2)}) copy-start(f32[512]{0:T(512)} %get-tuple-element.328) | copy-start | bytes 6148
  490.2 23.4 %copy-start.54 = (f32[512]{0:T(512)S(1)}, f32[512]{0:T(512)}, u32[]{:S(2)}) copy-start(f32[512]{0:T(512)} %get-tuple-element.251) | copy-start | bytes 6148
  490.2 23.4 %copy-start.55 = (f32[512]{0:T(512)S(1)}, f32[512]{0:T(512)}, u32[]{:S(2)}) copy-start(f32[512]{0:T(512)} %get-tuple-element.255) | copy-start | bytes 6148
  692.0 6.9 copy-start.41
  692.0 7.6 %copy-start.32 = (f32[512,512]{1,0:T(8,128)S(1)}, f32[512,512]{1,0:T(8,128)}, u32[]{:S(2)}) copy-start(f32[512,512]{1,0:T(8,128)} %get-tuple-element.594) | copy-start | bytes 3145732
  693.8 6.8 copy-start.31
  (32 other events, 42.2 us)
Sparse Core Ops, SparseCore 0:
  45.5 33.4 reduce-scatter.20
  81.7 31.4 reduce-scatter.18
  115.9 16.7 all-gather.8
  135.5 31.4 reduce-scatter.22
  169.0 16.7 all-gather.10
  194.5 31.4 reduce-scatter.24
  228.2 16.7 all-gather.12
  247.8 31.4 reduce-scatter.26
  285.9 16.7 all-gather.14
  304.7 16.7 all-gather.16
  330.8 24.8 reduce-scatter.28
  385.0 31.4 reduce-scatter.10
  419.1 31.3 reduce-scatter.12
  453.3 16.7 all-gather.6
  474.2 31.4 reduce-scatter.16
  508.2 31.5 reduce-scatter.14
  546.0 145.9 all-reduce.4
